TPU v7x, 32 devices: a whole 2x2x4 slice. The times are simulated.
32 devices in a mesh: shard: 16 (over z, y, x), head: 2 (over core).
Axes of the slice: x: 2, y: 2, z: 4, core: 2. Of those that a mesh axis runs over, the one named last changes fastest.
Arguments:
- queries: bfloat16 [8192, 2048], P('shard', 'head'), may hold values from -170 to 170
- key_weight: bfloat16 [1024, 2048], P('shard', 'head'), may hold values from -0.1875 to 0.1875
- value_weight: bfloat16 [1024, 2048], P('shard', 'head'), may hold values from -0.1875 to 0.1875
- out_weight: bfloat16 [4096, 2048], P(None, 'head'), may hold values from -0.5 to 0.5
- database: bfloat16 [64, 128, 1024], P('shard', 'head'), may hold values from -6 to 6
- neighbours: int32 [128, 2], replicated, may hold values from 0 to 63, as said below
- placement: int32 [64], replicated, may hold values from 0 to 63, as said below
Outputs:
- mixed: bfloat16 [8192, 4096], P('shard', 'head')
Inputs may be any that keep to these rules, and one draw needn't show every extreme that they name: `placement`: each storage slot appears once; slot s is stored on index s // 4 of shard. The 16 neighbours of the groups of one index of shard have storage slots on pairwise different indices of shard.
All inputs are finite; a program needn't handle non-finite values.
Results may differ from a plain program's by a relative error of at most 0.012.
The roundings to bfloat16 on the way count: a program that leaves them out, or rounds other values in their place, can miss the bound.
Values may be sent and summed in bfloat16 or wider, within the bound.
A program may use at most 128 MiB of HBM per device.

v0:
```python
import jax
import jax.numpy as jnp
from jax import lax
from jax.sharding import PartitionSpec as P

HD = 128
CH = 64
KNB = 2


def local(queries, key_weight, value_weight, out_weight, database, neighbours, placement):
    shard_count = lax.axis_size("shard")
    shard_self = lax.axis_index("shard")
    tok_rows = queries.shape[0]
    hd_local = queries.shape[1]
    heads_local = hd_local // HD
    per_dev = tok_rows // CH
    blk_local = database.shape[0]
    slots = placement[neighbours]
    needed = slots.reshape(shard_count, per_dev * KNB)
    owners = needed // blk_local
    matches = owners == shard_self
    hits = jnp.any(matches, axis=1)
    which = jnp.sum(jnp.where(matches, needed % blk_local, 0), axis=1)
    outgoing = jnp.where(hits[:, None, None], database[which], jnp.zeros((), jnp.bfloat16))
    arrived = lax.all_to_all(outgoing, "shard", split_axis=0, concat_axis=0, tiled=True)
    own_need = lax.dynamic_slice_in_dim(needed, shard_self, 1, 0)[0]
    half_rows = arrived[own_need // blk_local]
    encoded = lax.all_gather(half_rows, "head", axis=1, tiled=True)
    key_rows, val_rows = (
        lax.all_gather(key_weight, "shard", axis=0, tiled=True),
        lax.all_gather(value_weight, "shard", axis=0, tiled=True),
    )
    key_block = jnp.einsum(
        "brd,de->bre", encoded, key_rows, preferred_element_type=jnp.float32
    ).astype(jnp.bfloat16)
    val_block = jnp.einsum(
        "brd,de->bre", encoded, val_rows, preferred_element_type=jnp.float32
    ).astype(jnp.bfloat16)
    neighbour_len = encoded.shape[1]
    key_heads = key_block.reshape(per_dev, KNB * neighbour_len, heads_local, HD)
    val_heads = val_block.reshape(per_dev, KNB * neighbour_len, heads_local, HD)
    query_pad = jnp.concatenate(
        [queries[CH - 1 :], jnp.zeros((CH - 1, hd_local), jnp.bfloat16)], axis=0
    )
    query_pad = query_pad.reshape(per_dev, CH, heads_local, HD)
    score_scale = HD ** (-0.5)
    scores = (
        jnp.einsum("swhd,skhd->shwk", query_pad, key_heads, preferred_element_type=jnp.float32)
        * score_scale
    )
    row_max = jnp.max(scores, axis=-1, keepdims=True)
    expo = jnp.exp(scores - row_max)
    probs = expo / jnp.sum(expo, axis=-1, keepdims=True)
    weights_bf = probs.astype(jnp.bfloat16)
    window_out = jnp.einsum(
        "shwk,skhd->swhd", weights_bf, val_heads, preferred_element_type=jnp.float32
    )
    window_rows = window_out.astype(jnp.bfloat16).reshape(tok_rows, hd_local)
    attention = jnp.concatenate(
        [jnp.zeros((CH - 1, hd_local), jnp.bfloat16), window_rows[: tok_rows - (CH - 1)]], axis=0
    )
    partial_value = lax.dot_general(
        attention, out_weight, (((1,), (1,)), ((), ())), preferred_element_type=jnp.float32
    )
    return lax.psum_scatter(partial_value, "head", scatter_dimension=1, tiled=True).astype(
        jnp.bfloat16
    )


def solution(mesh):
    return jax.shard_map(
        local,
        mesh=mesh,
        in_specs=(
            P("shard", "head"),
            P("shard", "head"),
            P("shard", "head"),
            P(None, "head"),
            P("shard", "head", None),
            P(),
            P(),
        ),
        out_specs=P("shard", "head"),
        check_vma=False,
    )
```

profile of v0, /device:TPU:0, one launch (start us, length us, event | category | flops | bytes accessed | tf_op | source)
XLA Modules:
  0.0 240.5 jit_solution(13576988124075313294)
XLA Ops:
  6.5 0.8 compare_select_fusion
  7.6 1.9 gather_fusion
  10.1 0.7 gather_fusion.1
  10.9 1.5 broadcast_select_fusion
  12.4 8.3 %all-to-all-start = ((bf16[16,64,1024]{2,1,0:T(8,128)(2,1)}), bf16[16,64,1024]{2,1,0:T(8,128)(2,1)S(1)}, u32[]{:S(2)}, u32[]{:S(2)}) async-start(bf16[16,64,1024]{2,1,0:T(8,128)(2,1)} %broadcast_select_fusion), calls=%async_computation | async-start | bytes 4194304 | tf_op jit(solution)/shard_map/all_to_all | solution.py:26
  21.6 45.8 %all-to-all-done = bf16[16,64,1024]{2,1,0:T(8,128)(2,1)S(1)} async-done(((bf16[16,64,1024]{2,1,0:T(8,128)(2,1)}), bf16[16,64,1024]{2,1,0:T(8,128)(2,1)S(1)}, u32[]{:S(2)}, u32[]{:S(2)}) %all-to-all-start) | async-done | bytes 2097184 | tf_op jit(solution)/shard_map/all_to_all | solution.py:26
  67.4 2.0 gather_fusion.2
  69.5 0.7 all-gather.7.cloned.1.call-update
  70.2 1.4 slice.6
  72.1 27.0 %all-gather.5.cloned.1.call-done = bf16[1024,1024]{1,0:T(8,128)(2,1)} async-done(((bf16[64,1024]{1,0:T(8,128)(2,1)}), bf16[1024,1024]{1,0:T(8,128)(2,1)}) %all-gather.5.cloned.1.call-update) | async-done | bytes 2097168 | tf_op jit(solution)/shard_map/all_gather | solution.py:32
  99.0 13.9 %all-gather.9.cloned.1.call-done = bf16[16,128,1024]{2,1,0:T(8,128)(2,1)} async-done(((bf16[16,64,1024]{2,1,0:T(8,128)(2,1)}), bf16[16,128,1024]{2,1,0:T(8,128)(2,1)}) %all-gather.9.cloned.1.call-update) | async-done | bytes 4194320 | tf_op jit(solution)/shard_map/all_gather | solution.py:29
  112.9 7.4 %convolution_convert_fusion.1 = bf16[16,128,1024]{2,1,0:T(8,128)(2,1)S(1)} fusion(bf16[16,128,1024]{2,1,0:T(8,128)(2,1)} %all-gather.9.cloned.1.call-done, bf16[1024,1024]{1,0:T(8,128)(2,1)} %all-gather.5.cloned.1.call-done), kind=kOutput, calls=%fused_computation.13 | convolution fusion | flops 4297064448 | bytes 10485760 | tf_op jit(solution)/shard_map/brd,de->bre/dot_general | solution.py:37
  120.3 3.1 %copy.30 = bf16[256,8,8,128]{3,2,1,0:T(8,128)(2,1)} copy(bf16[256,8,8,128]{3,1,2,0:T(8,128)(2,1)S(1)} %bitcast.48) | data formatting | bytes 8388608
  123.4 54.2 %all-gather.7.cloned.1.call-done = bf16[1024,1024]{1,0:T(8,128)(2,1)} async-done(((bf16[64,1024]{1,0:T(8,128)(2,1)}), bf16[1024,1024]{1,0:T(8,128)(2,1)}) %all-gather.7.cloned.1.call-update) | async-done | bytes 2097168 | tf_op jit(solution)/shard_map/all_gather | solution.py:31
  177.6 7.4 %convolution_convert_fusion = bf16[16,128,1024]{2,1,0:T(8,128)(2,1)S(1)} fusion(bf16[16,128,1024]{2,1,0:T(8,128)(2,1)} %all-gather.9.cloned.1.call-done, bf16[1024,1024]{1,0:T(8,128)(2,1)} %all-gather.7.cloned.1.call-done), kind=kOutput, calls=%fused_computation.12 | convolution fusion | flops 4297064448 | bytes 10485760 | tf_op jit(solution)/shard_map/brd,de->bre/dot_general | solution.py:34
  185.0 1.1 copy.29
  186.1 1.6 fusion.3
  187.7 1.9 copy-done.3
  189.6 1.8 fusion.37
  191.4 11.9 %fusion.15 = bf16[8,64,8,128]{3,1,2,0:T(8,128)(2,1)S(1)} fusion(bf16[8,256,8,128]{3,2,1,0:T(8,128)(2,1)} %bitcast.46, f32[8,8,64]{2,1,0:T(8,128)S(1)} %fusion.37, f32[8,8,64,256]{3,2,1,0:T(8,128)} %copy-done.3), kind=kOutput, calls=%fused_computation.20 | convolution fusion | flops 274206976 | bytes 9453568 | tf_op jit(solution)/shard_map/shwk,skhd->swhd/dot_general | solution.py:56
  203.3 0.7 copy.27
  204.4 10.1 %fusion.19 = f32[512,4096]{1,0:T(8,128)} fusion(bf16[4096,1024]{1,0:T(8,128)(2,1)} %param.10, bf16[449,1024]{1,0:T(8,128)(2,1)S(1)} %slice.14), kind=kOutput, calls=%fused_computation.23 | convolution fusion | flops 4294967296 | bytes 17696768 | tf_op jit(solution)/shard_map/dot_general | solution.py:63
  214.5 15.6 %reduce-scatter.2.cloned.1.call-done = f32[512,2048]{1,0:T(8,128)} async-done(((f32[512,4096]{1,0:T(8,128)}), f32[512,2048]{1,0:T(8,128)}) %reduce-scatter.2.cloned.1.call-update) | async-done | bytes 4194320 | tf_op jit(solution)/shard_map/reduce_scatter | solution.py:66
  230.1 3.8 %convert_element_type.23 = bf16[512,2048]{1,0:T(8,128)(2,1)} convert(f32[512,2048]{1,0:T(8,128)} %reduce-scatter.2.cloned.1.call-done) | non-fusion elementwise | flops 1048576 | bytes 6291456 | tf_op jit(solution)/shard_map/convert_element_type | solution.py:66
  (34 shorter events, 2.7 us)
Async XLA Ops:
  6.5 3.5 %copy-start = (bf16[4,64,1024]{2,1,0:T(8,128)(2,1)S(1)}, bf16[4,64,1024]{2,1,0:T(8,128)(2,1)}, u32[]{:S(2)}) copy-start(bf16[4,64,1024]{2,1,0:T(8,128)(2,1)} %param.11) | copy-start | bytes 1572868
  6.5 1.0 copy-start.2
  12.4 55.0 %all-to-all-start = ((bf16[16,64,1024]{2,1,0:T(8,128)(2,1)}), bf16[16,64,1024]{2,1,0:T(8,128)(2,1)S(1)}, u32[]{:S(2)}, u32[]{:S(2)}) async-start(bf16[16,64,1024]{2,1,0:T(8,128)(2,1)} %broadcast_select_fusion), calls=%async_computation | async-start | bytes 4194304 | tf_op jit(solution)/shard_map/all_to_all | solution.py:26
  20.7 78.3 %all-gather.5.cloned.1.call-start = ((), (), s32[]{:S(2)}) async-start(), calls=%async_computation.2 | async-start | bytes 2228224 | tf_op jit(solution)/shard_map/all_gather | solution.py:32
  21.5 91.5 %all-gather.9.cloned.1.call-start = ((), (), s32[]{:S(2)}) async-start(), calls=%async_computation.5 | async-start | bytes 6291456 | tf_op jit(solution)/shard_map/all_gather | solution.py:29
  69.4 108.2 %all-gather.7.cloned.1.call-start = ((), (), s32[]{:S(2)}) async-start(), calls=%async_computation.3 | async-start | bytes 2228224 | tf_op jit(solution)/shard_map/all_gather | solution.py:31
  70.2 160.0 %reduce-scatter.2.cloned.1.call-start = ((), (), s32[]{:S(2)}) async-start(), calls=%async_computation.4 | async-start | bytes 12582912 | tf_op jit(solution)/shard_map/reduce_scatter | solution.py:66
  187.7 1.9 copy-start.3
  214.5 19.5 %copy-start.1 = (bf16[4,64,1024]{2,1,0:T(8,128)(2,1)S(1)}, bf16[4,64,1024]{2,1,0:T(8,128)(2,1)}, u32[]{:S(2)}) copy-start(bf16[4,64,1024]{2,1,0:T(8,128)(2,1)} %param.11) | copy-start | bytes 1572868
Sparse Core Ops, SparseCore 0:
  24.3 74.6 all-gather.4
  100.6 12.3 all-gather.8
  115.7 61.8 all-gather.6
  214.6 15.4 reduce-scatter.1
where the time goes:
time: 241 us
  waiting for transfers between devices  158 us (66%)
  matrix products  38.4 us (16%)
  local copies, waits for them, and re-layouts  14.2 us (6%)
  between operations  13.3 us (6%)
  starting transfers between devices  8.47 us (4%)
  other arithmetic  8.21 us (3%)
    all_gather x1, waiting for transfers between devices, local(): lax.all_gather(key_weight, 'shard', axis=0, tiled=True)  54.2 us
    all_to_all x1, waiting for transfers between devices, local(): lax.all_to_all(outgoing, 'shard', split_axis=0, concat_axis=0, tiled=True)  45.8 us
    all_gather x1, waiting for transfers between devices, local(): lax.all_gather(value_weight, 'shard', axis=0, tiled=True)  27 us
    reduce_scatter x1, waiting for transfers between devices, local(): lax.psum_scatter(partial_value, 'head', scatter_dimension=1, tiled=True)  15.6 us
    all_gather x1, waiting for transfers between devices, local(): encoded = lax.all_gather(half_rows, 'head', axis=1, tiled=True)  13.9 us
    dot_general x1, matrix products, local(): jnp.einsum('shwk,skhd->swhd', weights_bf, val_heads, preferred_element_ty...  11.9 us
    dot_general x1, matrix products, local(): lax.dot_general(attention, out_weight, (((1,), (1,)), ((), ())), preferre...  10.1 us
    all_to_all x1, starting transfers between devices, local(): lax.all_to_all(outgoing, 'shard', split_axis=0, concat_axis=0, tiled=True)  8.31 us
  transfers between devices with their start and end apart: 5, of which 5 were waited for; matrix products, arithmetic and copies ran while one was open for 6% of the time, Pallas kernels for 0%

commit v1 on v0

--- a/solution.py
+++ b/solution.py
@@ -1,14 +1,327 @@
 import jax
 import jax.numpy as jnp
 from jax import lax
+from jax.experimental import pallas as pl
+from jax.experimental.pallas import tpu as pltpu
 from jax.sharding import PartitionSpec as P
 
 HD = 128
 CH = 64
 KNB = 2
-
-
-def local(queries, key_weight, value_weight, out_weight, database, neighbours, placement):
+NZ, NY, NX = 4, 2, 2
+MESH = pl.DeviceIdType.MESH
+VMEM_LIMIT = 60 * 1024 * 1024
+NT = (((1,), (1,)), ((), ()))
+
+
+def shifted(shard, dz, dy, dx):
+    z, y, x = shard // (NY * NX), (shard // NX) % NY, shard % NX
+    return ((z + dz) % NZ) * (NY * NX) + ((y + dy) % NY) * NX + (x + dx) % NX
+
+
+def fused_kernel(
+    which_ref, slot_ref, q_ref, kw_ref, vw_ref, ow_ref, db_ref,
+    att_ref, ow_recv,
+    w, e_out, e_in, kk, vv,
+    a_send, a_recv, f_send, f_recv, z_send, p_send, g_send, w_recv, o_sem, t_send, t_recv,
+):
+    s = lax.axis_index("shard")
+    h = lax.axis_index("head")
+    z, y, x = s // (NY * NX), (s // NX) % NY, s % NX
+    near_x = s + 1 - 2 * x
+    near_y = s + NX * (1 - 2 * y)
+    plane = NY * NX
+    n = NZ * NY * NX
+    half, de = db_ref.shape[1], db_ref.shape[2]
+    width = q_ref.shape[1]
+    feats = ow_recv.shape[0]
+
+    barrier = pltpu.get_barrier_semaphore()
+    for d in range(1, n):
+        to = shifted(s, d // plane, (d // NX) % NY, d % NX)
+        pl.semaphore_signal(barrier, inc=1, device_id=(to, h), device_id_type=MESH)
+    pl.semaphore_signal(barrier, inc=1, device_id=(s, 1 - h), device_id_type=MESH)
+    w[0, s] = kw_ref[...]
+    w[1, s] = vw_ref[...]
+    for d in range(1, n):
+        e_out[d] = db_ref[which_ref[d]]
+    e_in[0, h] = db_ref[which_ref[0]]
+    pl.semaphore_wait(barrier, n)
+
+    def weight_copy(kind, chunk, to, sem):
+        return pltpu.make_async_remote_copy(
+            src_ref=w.at[kind, chunk], dst_ref=w.at[kind, chunk], send_sem=sem,
+            recv_sem=w_recv.at[kind, chunk], device_id=(to, h), device_id_type=MESH)
+
+    def up_copy(kind, zz):
+        return weight_copy(kind, zz * plane + y * NX + x, s + plane, z_send.at[0, kind, zz])
+
+    def down_copy(kind, zz):
+        return weight_copy(kind, zz * plane + y * NX + x, s - plane, z_send.at[1, kind, zz])
+
+    def x_copy(kind, zz):
+        return weight_copy(kind, zz * plane + y * NX + x, near_x, p_send.at[0, kind, zz])
+
+    def y_copy(kind, zz):
+        return weight_copy(kind, zz * plane + y * NX + x, near_y, p_send.at[1, kind, zz])
+
+    def diag_k(zz):
+        return weight_copy(0, zz * plane + y * NX + 1 - x, near_y, g_send.at[0, zz])
+
+    def diag_v(zz):
+        return weight_copy(1, zz * plane + (1 - y) * NX + x, near_x, g_send.at[1, zz])
+
+    def arrive(kind, chunk):
+        weight_copy(kind, chunk, near_x, z_send.at[0, 0, 0]).wait_recv()
+
+    def enc_copy(d):
+        to = shifted(s, d // plane, (d // NX) % NY, d % NX)
+        return pltpu.make_async_remote_copy(
+            src_ref=e_out.at[d], dst_ref=e_in.at[d, h], send_sem=a_send.at[d],
+            recv_sem=a_recv.at[d], device_id=(to, h), device_id_type=MESH)
+
+    def half_copy(d):
+        return pltpu.make_async_remote_copy(
+            src_ref=e_in.at[d, h], dst_ref=e_in.at[d, h], send_sem=f_send.at[d],
+            recv_sem=f_recv.at[d], device_id=(s, 1 - h), device_id_type=MESH)
+
+    def half_arrive(d):
+        pltpu.make_async_remote_copy(
+            src_ref=e_in.at[d, 1 - h], dst_ref=e_in.at[d, 1 - h], send_sem=f_send.at[d],
+            recv_sem=f_recv.at[d], device_id=(s, 1 - h), device_id_type=MESH).wait_recv()
+
+    def out_copy():
+        return pltpu.make_async_remote_copy(
+            src_ref=ow_ref.at[pl.ds((1 - h) * feats, feats), :], dst_ref=ow_recv,
+            send_sem=o_sem.at[0], recv_sem=o_sem.at[1], device_id=(s, 1 - h),
+            device_id_type=MESH)
+
+    for kind in range(2):
+        @pl.when(z < NZ - 1)
+        def _():
+            up_copy(kind, z).start()
+
+        @pl.when(z > 0)
+        def _():
+            down_copy(kind, z).start()
+        x_copy(kind, z).start()
+        y_copy(kind, z).start()
+    for dz in (2, 1, 3, 0):
+        for d in range(dz * plane, (dz + 1) * plane):
+            if d:
+                enc_copy(d).start()
+    half_copy(0).start()
+    out_copy().start()
+
+    def turn(zz):
+        arrive(0, zz * plane + y * NX + 1 - x)
+        diag_k(zz).start()
+        arrive(1, zz * plane + (1 - y) * NX + x)
+        diag_v(zz).start()
+
+    def pass_halves(dz):
+        for d in range(dz * plane, (dz + 1) * plane):
+            if d:
+                enc_copy(d).wait_recv()
+                half_copy(d).start()
+
+    for k in range(1, NZ + 1):
+        if k < NZ:
+            @pl.when(z >= k)
+            def _():
+                for kind in range(2):
+                    arrive(kind, (z - k) * plane + y * NX + x)
+
+                    @pl.when(z < NZ - 1)
+                    def _():
+                        up_copy(kind, z - k).start()
+                    x_copy(kind, z - k).start()
+                    y_copy(kind, z - k).start()
+
+            @pl.when(z + k < NZ)
+            def _():
+                for kind in range(2):
+                    arrive(kind, (z + k) * plane + y * NX + x)
+
+                    @pl.when(z > 0)
+                    def _():
+                        down_copy(kind, z + k).start()
+                    x_copy(kind, z + k).start()
+                    y_copy(kind, z + k).start()
+        if k == 1:
+            turn(z)
+        else:
+            @pl.when(z >= k - 1)
+            def _():
+                turn(z - (k - 1))
+
+            @pl.when(z + k - 1 < NZ)
+            def _():
+                turn(z + k - 1)
+    for zz in range(NZ):
+        arrive(1, zz * plane + y * NX + 1 - x)
+        arrive(0, zz * plane + (1 - y) * NX + x)
+        for kind in range(2):
+            arrive(kind, zz * plane + (1 - y) * NX + 1 - x)
+
+    order = (0, 1, 3, 2)
+    tile = 256
+    pass_halves(order[0])
+    for i, dz in enumerate(order):
+        if i + 1 < NZ:
+            pass_halves(order[i + 1])
+        for d in range(dz * plane, (dz + 1) * plane):
+            half_arrive(d)
+
+        @pl.loop(0, width // tile)
+        def _(c):
+            cols = pl.ds(pl.multiple_of(c * tile, tile), tile)
+            enc = e_in[dz * plane:(dz + 1) * plane].reshape(plane * 2 * half, de)
+            for kind, dst in ((0, kk), (1, vv)):
+                rows = w[kind, :, :, cols].reshape(de, tile)
+                got = jnp.dot(enc, rows, preferred_element_type=jnp.float32)
+                dst[dz * plane:(dz + 1) * plane, :, cols] = got.astype(jnp.bfloat16).reshape(
+                    plane, 2 * half, tile)
+
+    scale = HD ** -0.5
+    groups = q_ref.shape[0] // CH
+    edge = 16
+
+    def attend(c, start, count):
+        one = slot_ref[KNB * c]
+        two = slot_ref[KNB * c + 1]
+        for head in range(width // HD):
+            cols = slice(head * HD, (head + 1) * HD)
+            q = q_ref[pl.ds(start, count), cols]
+            score = jnp.concatenate(
+                [lax.dot_general(q, kk[one, :, cols], NT, preferred_element_type=jnp.float32),
+                 lax.dot_general(q, kk[two, :, cols], NT, preferred_element_type=jnp.float32)],
+                axis=1) * scale
+            expo = jnp.exp(score - jnp.max(score, axis=1, keepdims=True))
+            weight = (expo / jnp.sum(expo, axis=1, keepdims=True)).astype(jnp.bfloat16)
+            value = jnp.concatenate([vv[one, :, cols], vv[two, :, cols]], axis=0)
+            got = jnp.dot(weight, value, preferred_element_type=jnp.float32)
+            last = lax.broadcasted_iota(jnp.int32, (edge, HD), 0) == edge - 1
+            old = att_ref[0, pl.ds(start, edge), cols].astype(jnp.float32)
+            att_ref[0, pl.ds(start, edge), cols] = jnp.where(last, got[:edge], old).astype(jnp.bfloat16)
+            if count > edge:
+                att_ref[0, pl.ds(pl.multiple_of(start + edge, edge), count - edge), cols] = (
+                    got[edge:].astype(jnp.bfloat16))
+
+    def swap(c):
+        rows = pl.ds(pl.multiple_of(c * CH, CH), CH)
+        return pltpu.make_async_remote_copy(
+            src_ref=att_ref.at[0, rows], dst_ref=att_ref.at[1, rows], send_sem=t_send.at[c],
+            recv_sem=t_recv.at[c], device_id=(s, 1 - h), device_id_type=MESH)
+
+    att_ref[0, 0:CH] = jnp.zeros((CH, width), jnp.bfloat16)
+
+    @pl.loop(0, groups - 1)
+    def _(c):
+        attend(c, pl.multiple_of(c * CH + CH - edge, edge), CH + edge)
+        swap(c).start()
+
+    attend(groups - 1, groups * CH - edge, edge)
+    swap(groups - 1).start()
+
+    for zz in range(NZ):
+        for kind in range(2):
+            @pl.when(z < NZ - 1)
+            def _():
+                @pl.when(z >= zz)
+                def _():
+                    up_copy(kind, zz).wait_send()
+
+            @pl.when(z > 0)
+            def _():
+                @pl.when(z <= zz)
+                def _():
+                    down_copy(kind, zz).wait_send()
+            x_copy(kind, zz).wait_send()
+            y_copy(kind, zz).wait_send()
+        diag_k(zz).wait_send()
+        diag_v(zz).wait_send()
+    for d in range(n):
+        if d:
+            enc_copy(d).wait_send()
+        half_copy(d).wait_send()
+    out_copy().wait()
+    for c in range(groups):
+        swap(c).wait()
+
+
+def project_kernel(side_ref, att_ref, own_ref, other_ref, out_ref):
+    out_ref[...] = (
+        lax.dot_general(att_ref[0], own_ref[...], NT, preferred_element_type=jnp.float32)
+        + lax.dot_general(att_ref[1], other_ref[...], NT, preferred_element_type=jnp.float32)
+    ).astype(jnp.bfloat16)
+
+
+def local_small(queries, key_weight, value_weight, out_weight, database, neighbours, placement):
+    n = NZ * NY * NX
+    s = lax.axis_index("shard")
+    h = lax.axis_index("head")
+    tok, width = queries.shape
+    blk, half, de = database.shape
+    feats = out_weight.shape[0] // 2
+    nblocks = placement.shape[0]
+    ids = jnp.arange(nblocks, dtype=jnp.int32)
+    needed = neighbours.reshape(n, -1)
+    slots = jnp.sum(jnp.where(needed[:, :, None] == ids, placement, 0), axis=-1)
+    owners = slots // blk
+    offs = jnp.arange(n, dtype=jnp.int32)
+    dests = shifted(s, offs // (NY * NX), (offs // NX) % NY, offs % NX)
+    pick = (dests[:, None, None] == offs[None, :, None]) & (owners == s)[None]
+    which = jnp.sum(jnp.where(pick, (slots % blk)[None], 0), axis=(1, 2))
+    own = jnp.sum(jnp.where((offs == s)[:, None], owners, 0), axis=0)
+    slot = (
+        ((s // 4 - own // 4) % NZ) * 4 + ((s // 2 - own // 2) % NY) * 2 + (s - own) % NX
+    ).astype(jnp.int32)
+    vm = pl.BlockSpec(memory_space=pltpu.VMEM)
+    sm = pl.BlockSpec(memory_space=pltpu.SMEM)
+    hbm = pl.BlockSpec(memory_space=pl.ANY)
+    dma = pltpu.SemaphoreType.DMA
+    att, ow_recv = pl.pallas_call(
+        fused_kernel,
+        out_shape=(
+            jax.ShapeDtypeStruct((2, tok, width), jnp.bfloat16),
+            jax.ShapeDtypeStruct((feats, width), jnp.bfloat16),
+        ),
+        in_specs=[sm, sm, vm, vm, vm, hbm, vm],
+        out_specs=(vm, hbm),
+        scratch_shapes=[
+            pltpu.VMEM((2, n) + key_weight.shape, jnp.bfloat16),
+            pltpu.VMEM((n, half, de), jnp.bfloat16),
+            pltpu.VMEM((n, 2, half, de), jnp.bfloat16),
+            pltpu.VMEM((n, 2 * half, width), jnp.bfloat16),
+            pltpu.VMEM((n, 2 * half, width), jnp.bfloat16),
+            dma((n,)), dma((n,)), dma((n,)), dma((n,)),
+            dma((2, 2, NZ)), dma((2, 2, NZ)), dma((2, NZ)), dma((2, n)),
+            dma((2,)), dma((tok // CH,)), dma((tok // CH,)),
+        ],
+        compiler_params=pltpu.CompilerParams(
+            collective_id=0, has_side_effects=True, vmem_limit_bytes=VMEM_LIMIT),
+    )(which.astype(jnp.int32), slot, queries, key_weight, value_weight, out_weight, database)
+    tile = 256
+    steps = feats // tile
+    return pl.pallas_call(
+        project_kernel,
+        out_shape=jax.ShapeDtypeStruct((tok, feats), jnp.bfloat16),
+        grid_spec=pltpu.PrefetchScalarGridSpec(
+            num_scalar_prefetch=1,
+            grid=(steps,),
+            in_specs=[
+                pl.BlockSpec((2, tok, width), lambda i, side: (0, 0, 0)),
+                pl.BlockSpec((tile, width), lambda i, side: (side[0] * steps + i, 0)),
+                pl.BlockSpec((tile, width), lambda i, side: (i, 0)),
+            ],
+            out_specs=pl.BlockSpec((tok, tile), lambda i, side: (0, i)),
+        ),
+        compiler_params=pltpu.CompilerParams(vmem_limit_bytes=VMEM_LIMIT),
+    )(h.astype(jnp.int32).reshape(1), att, out_weight, ow_recv)
+
+
+def local_general(queries, key_weight, value_weight, out_weight, database, neighbours, placement):
     shard_count = lax.axis_size("shard")
     shard_self = lax.axis_index("shard")
     tok_rows = queries.shape[0]
@@ -69,8 +382,10 @@
 
 
 def solution(mesh):
+    sizes = dict(mesh.shape)
+    small = sizes["shard"] == NZ * NY * NX and sizes["head"] == 2
     return jax.shard_map(
-        local,
+        local_small if small else local_general,
         mesh=mesh,
         in_specs=(
             P("shard", "head"),

time: 241 us -> 133 us (0.55)
  waiting for transfers between devices: 158 us -> 0 us
  Pallas kernels: 0 us -> 129 us
  matrix products: 38.4 us -> 0 us
  local copies, waits for them, and re-layouts: 14.2 us -> 0.87 us
  between operations: 13.3 us -> 0.02 us
  starting transfers between devices: 8.47 us -> 0 us
  other arithmetic: 8.21 us -> 2.81 us
    pallas_call x0 -> x2, Pallas kernels: none -> 129 us  [the longest x1 119 us: local_small(): pl.pallas_call(fused_kernel, out_shape=(jax.ShapeDtypeStruct((2, tok, wid...]
    all_gather x3 -> x0, waiting for transfers between devices: 95.1 us -> none  [the longest x1 54.2 us: local(): lax.all_gather(key_weight, 'shard', axis=0, tiled=True)]
    all_to_all x1 -> x0, waiting for transfers between devices: 45.8 us -> none  [local(): lax.all_to_all(outgoing, 'shard', split_axis=0, concat_axis=0, tiled=True)]
    dot_general x5 -> x0, matrix products: 38.4 us -> none  [the longest x1 11.9 us: local(): jnp.einsum('shwk,skhd->swhd', weights_bf, val_heads, preferred_element_ty...]
    reduce_scatter x1 -> x0, waiting for transfers between devices: 15.6 us -> none  [local(): lax.psum_scatter(partial_value, 'head', scatter_dimension=1, tiled=True)]
    all_to_all x1 -> x0, starting transfers between devices: 8.31 us -> none  [local(): lax.all_to_all(outgoing, 'shard', split_axis=0, concat_axis=0, tiled=True)]
    unnamed x13 -> x1, local copies, waits for them, and re-layouts: 6.76 us -> 0.78 us
    gather x5 -> x0, local copies, waits for them, and re-layouts: 4.74 us -> none  [the longest x3 2.06 us: local(): slots = placement[neighbours]]
  transfers between devices with their start and end apart: 5 -> 0, of which waited for: 5 -> 0; matrix products, arithmetic and copies ran while one was open for 6% -> 0% of each run, Pallas kernels for 0% -> 0%
where the time goes in v1:
time: 133 us
  Pallas kernels  129 us (97%)
  other arithmetic  2.81 us (2%)
    pallas_call x1, Pallas kernels, local_small(): pl.pallas_call(fused_kernel, out_shape=(jax.ShapeDtypeStruct((2, tok, wid...  119 us
    pallas_call x1, Pallas kernels, local_small(): pl.pallas_call(project_kernel, out_shape=jax.ShapeDtypeStruct((tok, feats...  10.6 us

profile of v1, /device:TPU:0, one launch (start us, length us, event | category | flops | bytes accessed | tf_op | source)
XLA Modules:
  0.0 133.1 jit_solution(12642255839632947005)
XLA Ops:
  0.0 0.8 copy.9
  0.8 0.1 eq.70
  0.9 1.1 select_reduce_fusion.1
  2.0 0.1 select_reduce_fusion.2
  2.1 0.5 fusion.3
  2.6 0.1 iota_compare_fusion.1
  2.7 1.0 select_reduce_fusion.which_ref
  3.7 118.8 %shard_map.73 = (bf16[2,512,1024]{2,1,0:T(8,128)(2,1)}, bf16[2048,1024]{1,0:T(8,128)(2,1)}) custom-call(s32[16]{0:T(128)} %select_reduce_fusion.which_ref, s32[16]{0:T(128)} %get-tuple-element.12.slot_ref, bf16[512,1024]{1,0:T(8,128)(2,1)} %q_ref.1, bf16[64,1024]{1,0:T(8,128)(2,1)} %kw_ref.1, bf16[64,1024]{1,0:T(8,128)(2,1)} %vw_ref.1, ...), custom_call_target="tpu_custom_call" | custom-call | tf_op jit(solution)/shard_map/pallas_call | solution.py:284
  122.5 10.6 %shard_map.74 = bf16[512,2048]{1,0:T(8,128)(2,1)} custom-call(s32[1]{0:T(128)} %bitcast.side_ref, bf16[2,512,1024]{2,1,0:T(8,128)(2,1)} %get-tuple-element.7.att_ref, bf16[4096,1024]{1,0:T(8,128)(2,1)} %own_ref.1, bf16[2048,1024]{1,0:T(8,128)(2,1)} %get-tuple-element.8.other_ref), custom_call_target="tpu_custom_call" | custom-call | tf_op jit(solution)/shard_map/pallas_call | solution.py:307
  (2 shorter events, 0.0 us)

commit v2 on v1

--- a/solution.py
+++ b/solution.py
@@ -22,8 +22,9 @@
 def fused_kernel(
     which_ref, slot_ref, q_ref, kw_ref, vw_ref, ow_ref, db_ref,
     att_ref, ow_recv,
-    w, e_out, e_in, kk, vv,
-    a_send, a_recv, f_send, f_recv, z_send, p_send, g_send, w_recv, o_sem, t_send, t_recv,
+    w, up_1, up_2, up_3, down_1, down_2, down_3, e_out, e_in, kk, vv,
+    d_send, d_recv, a_send, a_recv, f_send, f_recv, z_send, p_send, g_send, w_recv, o_sem,
+    t_send, t_recv,
 ):
     s = lax.axis_index("shard")
     h = lax.axis_index("head")
@@ -43,10 +44,9 @@
     pl.semaphore_signal(barrier, inc=1, device_id=(s, 1 - h), device_id_type=MESH)
     w[0, s] = kw_ref[...]
     w[1, s] = vw_ref[...]
-    for d in range(1, n):
-        e_out[d] = db_ref[which_ref[d]]
-    e_in[0, h] = db_ref[which_ref[0]]
     pl.semaphore_wait(barrier, n)
+    ups = (db_ref, up_1, up_2, up_3)
+    downs = (db_ref, down_1, down_2, down_3)
 
     def weight_copy(kind, chunk, to, sem):
         return pltpu.make_async_remote_copy(
@@ -74,11 +74,49 @@
     def arrive(kind, chunk):
         weight_copy(kind, chunk, near_x, z_send.at[0, 0, 0]).wait_recv()
 
-    def enc_copy(d):
-        to = shifted(s, d // plane, (d // NX) % NY, d % NX)
+    def set_up(k):
+        return pltpu.make_async_remote_copy(
+            src_ref=ups[k], dst_ref=ups[k + 1], send_sem=d_send.at[0, k],
+            recv_sem=d_recv.at[0, k + 1], device_id=(s + plane, h), device_id_type=MESH)
+
+    def set_down(k):
+        return pltpu.make_async_remote_copy(
+            src_ref=downs[k], dst_ref=downs[k + 1], send_sem=d_send.at[1, k],
+            recv_sem=d_recv.at[1, k + 1], device_id=(s - plane, h), device_id_type=MESH)
+
+    def enc_copy(zz, j):
+        to = shifted(s, 0, j // NX, j % NX)
+        d = zz * plane + j
         return pltpu.make_async_remote_copy(
             src_ref=e_out.at[d], dst_ref=e_in.at[d, h], send_sem=a_send.at[d],
             recv_sem=a_recv.at[d], device_id=(to, h), device_id_type=MESH)
+
+    def spread(zz, held):
+        for j in range(1, plane):
+            d = zz * plane + j
+            e_out[d] = held[which_ref[d]]
+            enc_copy(zz, j).start()
+        e_in[zz * plane, h] = held[which_ref[zz * plane]]
+        half_copy(zz * plane).start()
+
+    def sets(k):
+        @pl.when(z >= k)
+        def _():
+            set_up(k - 1).wait_recv()
+            if k < NZ - 1:
+                @pl.when(z < NZ - 1)
+                def _():
+                    set_up(k).start()
+            spread(z - k, ups[k])
+
+        @pl.when(z + k < NZ)
+        def _():
+            set_down(k - 1).wait_recv()
+            if k < NZ - 1:
+                @pl.when(z > 0)
+                def _():
+                    set_down(k).start()
+            spread(z + k, downs[k])
 
     def half_copy(d):
         return pltpu.make_async_remote_copy(
@@ -106,11 +144,7 @@
             down_copy(kind, z).start()
         x_copy(kind, z).start()
         y_copy(kind, z).start()
-    for dz in (2, 1, 3, 0):
-        for d in range(dz * plane, (dz + 1) * plane):
-            if d:
-                enc_copy(d).start()
-    half_copy(0).start()
+    spread(z, db_ref)
     out_copy().start()
 
     def turn(zz):
@@ -119,11 +153,10 @@
         arrive(1, zz * plane + (1 - y) * NX + x)
         diag_v(zz).start()
 
-    def pass_halves(dz):
-        for d in range(dz * plane, (dz + 1) * plane):
-            if d:
-                enc_copy(d).wait_recv()
-                half_copy(d).start()
+    def pass_halves(zz):
+        for j in range(1, plane):
+            enc_copy(zz, j).wait_recv()
+            half_copy(zz * plane + j).start()
 
     for k in range(1, NZ + 1):
         if k < NZ:
@@ -149,6 +182,13 @@
                     x_copy(kind, z + k).start()
                     y_copy(kind, z + k).start()
         if k == 1:
+            @pl.when(z < NZ - 1)
+            def _():
+                set_up(0).start()
+
+            @pl.when(z > 0)
+            def _():
+                set_down(0).start()
             turn(z)
         else:
             @pl.when(z >= k - 1)
@@ -158,30 +198,46 @@
             @pl.when(z + k - 1 < NZ)
             def _():
                 turn(z + k - 1)
+        if 2 <= k < NZ:
+            sets(k - 1)
     for zz in range(NZ):
         arrive(1, zz * plane + y * NX + 1 - x)
         arrive(0, zz * plane + (1 - y) * NX + x)
         for kind in range(2):
             arrive(kind, zz * plane + (1 - y) * NX + 1 - x)
 
-    order = (0, 1, 3, 2)
     tile = 256
-    pass_halves(order[0])
-    for i, dz in enumerate(order):
-        if i + 1 < NZ:
-            pass_halves(order[i + 1])
-        for d in range(dz * plane, (dz + 1) * plane):
-            half_arrive(d)
+
+    def project(zz):
+        for j in range(plane):
+            half_arrive(zz * plane + j)
+        slab = pl.ds(zz * plane, plane)
 
         @pl.loop(0, width // tile)
         def _(c):
             cols = pl.ds(pl.multiple_of(c * tile, tile), tile)
-            enc = e_in[dz * plane:(dz + 1) * plane].reshape(plane * 2 * half, de)
+            enc = e_in[slab].reshape(plane * 2 * half, de)
             for kind, dst in ((0, kk), (1, vv)):
                 rows = w[kind, :, :, cols].reshape(de, tile)
                 got = jnp.dot(enc, rows, preferred_element_type=jnp.float32)
-                dst[dz * plane:(dz + 1) * plane, :, cols] = got.astype(jnp.bfloat16).reshape(
-                    plane, 2 * half, tile)
+                dst[slab, :, cols] = got.astype(jnp.bfloat16).reshape(plane, 2 * half, tile)
+
+    def each(k, act):
+        @pl.when(z >= k)
+        def _():
+            act(z - k)
+
+        @pl.when(z + k < NZ)
+        def _():
+            act(z + k)
+
+    pass_halves(z)
+    project(z)
+    for k in range(1, NZ):
+        each(k, pass_halves)
+        if k == NZ - 2:
+            sets(NZ - 1)
+        each(k, project)
 
     scale = HD ** -0.5
     groups = q_ref.shape[0] // CH
@@ -190,23 +246,31 @@
     def attend(c, start, count):
         one = slot_ref[KNB * c]
         two = slot_ref[KNB * c + 1]
-        for head in range(width // HD):
-            cols = slice(head * HD, (head + 1) * HD)
-            q = q_ref[pl.ds(start, count), cols]
-            score = jnp.concatenate(
-                [lax.dot_general(q, kk[one, :, cols], NT, preferred_element_type=jnp.float32),
-                 lax.dot_general(q, kk[two, :, cols], NT, preferred_element_type=jnp.float32)],
-                axis=1) * scale
-            expo = jnp.exp(score - jnp.max(score, axis=1, keepdims=True))
-            weight = (expo / jnp.sum(expo, axis=1, keepdims=True)).astype(jnp.bfloat16)
-            value = jnp.concatenate([vv[one, :, cols], vv[two, :, cols]], axis=0)
-            got = jnp.dot(weight, value, preferred_element_type=jnp.float32)
-            last = lax.broadcasted_iota(jnp.int32, (edge, HD), 0) == edge - 1
-            old = att_ref[0, pl.ds(start, edge), cols].astype(jnp.float32)
-            att_ref[0, pl.ds(start, edge), cols] = jnp.where(last, got[:edge], old).astype(jnp.bfloat16)
-            if count > edge:
-                att_ref[0, pl.ds(pl.multiple_of(start + edge, edge), count - edge), cols] = (
-                    got[edge:].astype(jnp.bfloat16))
+        last = lax.broadcasted_iota(jnp.int32, (edge, HD), 0) == edge - 1
+        batch = 4
+        for first in range(0, width // HD, batch):
+            spans = [slice(i * HD, (i + 1) * HD) for i in range(first, first + batch)]
+            scores = []
+            for cols in spans:
+                q = q_ref[pl.ds(start, count), cols]
+                keys = jnp.concatenate([kk[one, :, cols], kk[two, :, cols]], axis=0)
+                scores.append(
+                    lax.dot_general(q, keys, NT, preferred_element_type=jnp.float32) * scale)
+            tops = [jnp.max(score, axis=1, keepdims=True) for score in scores]
+            expos = [jnp.exp(score - top) for score, top in zip(scores, tops)]
+            sums = [jnp.sum(expo, axis=1, keepdims=True) for expo in expos]
+            weights = [(expo / total).astype(jnp.bfloat16) for expo, total in zip(expos, sums)]
+            outs = []
+            for cols, weight in zip(spans, weights):
+                value = jnp.concatenate([vv[one, :, cols], vv[two, :, cols]], axis=0)
+                outs.append(jnp.dot(weight, value, preferred_element_type=jnp.float32))
+            for cols, got in zip(spans, outs):
+                old = att_ref[0, pl.ds(start, edge), cols].astype(jnp.float32)
+                att_ref[0, pl.ds(start, edge), cols] = jnp.where(last, got[:edge], old).astype(
+                    jnp.bfloat16)
+                if count > edge:
+                    att_ref[0, pl.ds(pl.multiple_of(start + edge, edge), count - edge), cols] = (
+                        got[edge:].astype(jnp.bfloat16))
 
     def swap(c):
         rows = pl.ds(pl.multiple_of(c * CH, CH), CH)
@@ -241,10 +305,23 @@
             y_copy(kind, zz).wait_send()
         diag_k(zz).wait_send()
         diag_v(zz).wait_send()
-    for d in range(n):
-        if d:
-            enc_copy(d).wait_send()
-        half_copy(d).wait_send()
+    for k in range(NZ - 1):
+        @pl.when(z < NZ - 1)
+        def _():
+            @pl.when(z >= k)
+            def _():
+                set_up(k).wait_send()
+
+        @pl.when(z > 0)
+        def _():
+            @pl.when(z + k < NZ)
+            def _():
+                set_down(k).wait_send()
+    for zz in range(NZ):
+        for j in range(plane):
+            if j:
+                enc_copy(zz, j).wait_send()
+            half_copy(zz * plane + j).wait_send()
     out_copy().wait()
     for c in range(groups):
         swap(c).wait()
@@ -270,12 +347,14 @@
     slots = jnp.sum(jnp.where(needed[:, :, None] == ids, placement, 0), axis=-1)
     owners = slots // blk
     offs = jnp.arange(n, dtype=jnp.int32)
-    dests = shifted(s, offs // (NY * NX), (offs // NX) % NY, offs % NX)
-    pick = (dests[:, None, None] == offs[None, :, None]) & (owners == s)[None]
+    plane = NY * NX
+    dests = shifted(s, 0, (offs // NX) % NY, offs % NX)
+    origin = offs // plane * plane + s % plane
+    pick = (dests[:, None, None] == offs[None, :, None]) & (owners[None] == origin[:, None, None])
     which = jnp.sum(jnp.where(pick, (slots % blk)[None], 0), axis=(1, 2))
     own = jnp.sum(jnp.where((offs == s)[:, None], owners, 0), axis=0)
     slot = (
-        ((s // 4 - own // 4) % NZ) * 4 + ((s // 2 - own // 2) % NY) * 2 + (s - own) % NX
+        own // plane * plane + (s // NX + own // NX) % NY * NX + (s + own) % NX
     ).astype(jnp.int32)
     vm = pl.BlockSpec(memory_space=pltpu.VMEM)
     sm = pl.BlockSpec(memory_space=pltpu.SMEM)
@@ -291,11 +370,12 @@
         out_specs=(vm, hbm),
         scratch_shapes=[
             pltpu.VMEM((2, n) + key_weight.shape, jnp.bfloat16),
+            *[pltpu.VMEM(database.shape, jnp.bfloat16)] * 6,
             pltpu.VMEM((n, half, de), jnp.bfloat16),
             pltpu.VMEM((n, 2, half, de), jnp.bfloat16),
             pltpu.VMEM((n, 2 * half, width), jnp.bfloat16),
             pltpu.VMEM((n, 2 * half, width), jnp.bfloat16),
-            dma((n,)), dma((n,)), dma((n,)), dma((n,)),
+            dma((2, NZ)), dma((2, NZ)), dma((n,)), dma((n,)), dma((n,)), dma((n,)),
             dma((2, 2, NZ)), dma((2, 2, NZ)), dma((2, NZ)), dma((2, n)),
             dma((2,)), dma((tok // CH,)), dma((tok // CH,)),
         ],

time: 133 us -> 105 us (0.79)
  Pallas kernels: 129 us -> 101 us
    pallas_call x1, Pallas kernels: 119 us -> 90.9 us  [local_small(): pl.pallas_call(fused_kernel, out_shape=(jax.ShapeDtypeStruct((2, tok, wid...]
where the time goes in v2:
time: 105 us
  Pallas kernels  101 us (96%)
  other arithmetic  2.84 us (3%)
    pallas_call x1, Pallas kernels, local_small(): pl.pallas_call(fused_kernel, out_shape=(jax.ShapeDtypeStruct((2, tok, wid...  90.9 us
    pallas_call x1, Pallas kernels, local_small(): pl.pallas_call(project_kernel, out_shape=jax.ShapeDtypeStruct((tok, feats...  10.6 us

profile of v2, /device:TPU:0, one launch (start us, length us, event | category | flops | bytes accessed | tf_op | source)
XLA Modules:
  0.0 105.2 jit_solution(16314200788432482578)
XLA Ops:
  0.0 0.1 iota_compare_fusion.1
  0.1 0.8 copy.9
  0.9 0.1 eq.73
  1.0 1.1 %select_reduce_fusion.1 = s32[16,16]{1,0:T(8,128)S(1)} fusion(s32[64]{0:T(128)} %param.13, s32[16,16]{1,0:T(8,128)S(1)} %eq.73), kind=kLoop, calls=%fused_computation.1 | loop fusion | flops 48896 | bytes 2304 | tf_op jit(solution)/shard_map/reduce_sum | solution.py:347
  2.1 0.1 select_reduce_fusion.2
  2.2 1.0 select_reduce_fusion.which_ref
  3.2 0.6 fusion.4.slot_ref
  3.7 90.9 %shard_map.73 = (bf16[2,512,1024]{2,1,0:T(8,128)(2,1)}, bf16[2048,1024]{1,0:T(8,128)(2,1)}) custom-call(s32[16]{0:T(128)} %select_reduce_fusion.which_ref, s32[16]{0:T(128)} %fusion.4.slot_ref, bf16[512,1024]{1,0:T(8,128)(2,1)} %q_ref.1, bf16[64,1024]{1,0:T(8,128)(2,1)} %kw_ref.1, bf16[64,1024]{1,0:T(8,128)(2,1)} %vw_ref.1, bf16[4096,1024]{1,0:T(8,128)(2,1)} %own_ref.1, ...), custom_call_target="tpu_custom_call" | custom-call | tf_op jit(solution)/shard_map/pallas_call | solution.py:363
  94.6 10.6 %shard_map.74 = bf16[512,2048]{1,0:T(8,128)(2,1)} custom-call(s32[1]{0:T(128)} %bitcast.side_ref, bf16[2,512,1024]{2,1,0:T(8,128)(2,1)} %get-tuple-element.7.att_ref, bf16[4096,1024]{1,0:T(8,128)(2,1)} %own_ref.1, bf16[2048,1024]{1,0:T(8,128)(2,1)} %get-tuple-element.8.other_ref), custom_call_target="tpu_custom_call" | custom-call | tf_op jit(solution)/shard_map/pallas_call | solution.py:387
  (3 shorter events, 0.0 us)

commit v3 on v2

--- a/solution.py
+++ b/solution.py
@@ -99,7 +99,7 @@
         e_in[zz * plane, h] = held[which_ref[zz * plane]]
         half_copy(zz * plane).start()
 
-    def sets(k):
+    def hand_on(k):
         @pl.when(z >= k)
         def _():
             set_up(k - 1).wait_recv()
@@ -107,7 +107,6 @@
                 @pl.when(z < NZ - 1)
                 def _():
                     set_up(k).start()
-            spread(z - k, ups[k])
 
         @pl.when(z + k < NZ)
         def _():
@@ -116,6 +115,14 @@
                 @pl.when(z > 0)
                 def _():
                     set_down(k).start()
+
+    def spread_sets(k):
+        @pl.when(z >= k)
+        def _():
+            spread(z - k, ups[k])
+
+        @pl.when(z + k < NZ)
+        def _():
             spread(z + k, downs[k])
 
     def half_copy(d):
@@ -144,7 +151,6 @@
             down_copy(kind, z).start()
         x_copy(kind, z).start()
         y_copy(kind, z).start()
-    spread(z, db_ref)
     out_copy().start()
 
     def turn(zz):
@@ -198,8 +204,12 @@
             @pl.when(z + k - 1 < NZ)
             def _():
                 turn(z + k - 1)
-        if 2 <= k < NZ:
-            sets(k - 1)
+        if k == 2:
+            hand_on(1)
+    spread(z, db_ref)
+    spread_sets(1)
+    hand_on(2)
+    spread_sets(2)
     for zz in range(NZ):
         arrive(1, zz * plane + y * NX + 1 - x)
         arrive(0, zz * plane + (1 - y) * NX + x)
@@ -236,7 +246,8 @@
     for k in range(1, NZ):
         each(k, pass_halves)
         if k == NZ - 2:
-            sets(NZ - 1)
+            hand_on(NZ - 1)
+            spread_sets(NZ - 1)
         each(k, project)
 
     scale = HD ** -0.5
@@ -382,7 +393,7 @@
         compiler_params=pltpu.CompilerParams(
             collective_id=0, has_side_effects=True, vmem_limit_bytes=VMEM_LIMIT),
     )(which.astype(jnp.int32), slot, queries, key_weight, value_weight, out_weight, database)
-    tile = 256
+    tile = 512
     steps = feats // tile
     return pl.pallas_call(
         project_kernel,

time: 105 us -> 103 us (0.981)
  Pallas kernels: 101 us -> 99.2 us
    pallas_call x1, Pallas kernels: 10.6 us -> 8.78 us  [local_small(): pl.pallas_call(project_kernel, out_shape=jax.ShapeDtypeStruct((tok, feats...]
where the time goes in v3:
time: 103 us
  Pallas kernels  99.2 us (96%)
  other arithmetic  2.84 us (3%)
    pallas_call x1, Pallas kernels, local_small(): pl.pallas_call(fused_kernel, out_shape=(jax.ShapeDtypeStruct((2, tok, wid...  90.4 us
    pallas_call x1, Pallas kernels, local_small(): pl.pallas_call(project_kernel, out_shape=jax.ShapeDtypeStruct((tok, feats...  8.78 us

profile of v3, /device:TPU:0, one launch (start us, length us, event | category | flops | bytes accessed | tf_op | source)
XLA Modules:
  0.0 102.9 jit_solution(5650813472426935068)
XLA Ops:
  0.0 0.1 iota_compare_fusion.1
  0.1 0.8 copy.9
  0.9 0.1 eq.73
  1.0 1.1 %select_reduce_fusion.1 = s32[16,16]{1,0:T(8,128)S(1)} fusion(s32[64]{0:T(128)} %param.13, s32[16,16]{1,0:T(8,128)S(1)} %eq.73), kind=kLoop, calls=%fused_computation.1 | loop fusion | flops 48896 | bytes 2304 | tf_op jit(solution)/shard_map/reduce_sum | solution.py:358
  2.1 0.1 select_reduce_fusion.2
  2.2 1.0 select_reduce_fusion.which_ref
  3.2 0.6 fusion.4.slot_ref
  3.7 90.4 %shard_map.73 = (bf16[2,512,1024]{2,1,0:T(8,128)(2,1)}, bf16[2048,1024]{1,0:T(8,128)(2,1)}) custom-call(s32[16]{0:T(128)} %select_reduce_fusion.which_ref, s32[16]{0:T(128)} %fusion.4.slot_ref, bf16[512,1024]{1,0:T(8,128)(2,1)} %q_ref.1, bf16[64,1024]{1,0:T(8,128)(2,1)} %kw_ref.1, bf16[64,1024]{1,0:T(8,128)(2,1)} %vw_ref.1, bf16[4096,1024]{1,0:T(8,128)(2,1)} %own_ref.1, ...), custom_call_target="tpu_custom_call" | custom-call | tf_op jit(solution)/shard_map/pallas_call | solution.py:374
  94.1 8.8 %shard_map.74 = bf16[512,2048]{1,0:T(8,128)(2,1)} custom-call(s32[1]{0:T(128)} %bitcast.side_ref, bf16[2,512,1024]{2,1,0:T(8,128)(2,1)} %get-tuple-element.7.att_ref, bf16[4096,1024]{1,0:T(8,128)(2,1)} %own_ref.1, bf16[2048,1024]{1,0:T(8,128)(2,1)} %get-tuple-element.8.other_ref), custom_call_target="tpu_custom_call" | custom-call | tf_op jit(solution)/shard_map/pallas_call | solution.py:398
  (3 shorter events, 0.0 us)

commit v4 on v3

--- a/solution.py
+++ b/solution.py
@@ -20,7 +20,7 @@
 
 
 def fused_kernel(
-    which_ref, slot_ref, q_ref, kw_ref, vw_ref, ow_ref, db_ref,
+    near_ref, place_ref, q_ref, kw_ref, vw_ref, ow_ref, db_ref,
     att_ref, ow_recv,
     w, up_1, up_2, up_3, down_1, down_2, down_3, e_out, e_in, kk, vv,
     d_send, d_recv, a_send, a_recv, f_send, f_recv, z_send, p_send, g_send, w_recv, o_sem,
@@ -94,9 +94,9 @@
     def spread(zz, held):
         for j in range(1, plane):
             d = zz * plane + j
-            e_out[d] = held[which_ref[d]]
+            e_out[d] = held[chosen(zz, j)]
             enc_copy(zz, j).start()
-        e_in[zz * plane, h] = held[which_ref[zz * plane]]
+        e_in[zz * plane, h] = held[chosen(zz, 0)]
         half_copy(zz * plane).start()
 
     def hand_on(k):
@@ -125,6 +125,24 @@
         def _():
             spread(z + k, downs[k])
 
+    picks = near_ref.shape[0] // n
+    blk = db_ref.shape[0]
+
+    def find(j):
+        to = shifted(s, 0, j // NX, j % NX)
+        found = [jnp.int32(0)] * NZ
+        for i in range(picks):
+            stored = place_ref[near_ref[to * picks + i]]
+            owner, block = stored // blk, stored % blk
+            found = [
+                got + jnp.where(owner == zz * plane + s % plane, block, 0)
+                for zz, got in enumerate(found)]
+        return found
+
+    def slot_of(i):
+        own = place_ref[near_ref[s * picks + i]] // blk
+        return own // plane * plane + (y + own // NX) % NY * NX + (x + own) % NX
+
     def half_copy(d):
         return pltpu.make_async_remote_copy(
             src_ref=e_in.at[d, h], dst_ref=e_in.at[d, h], send_sem=f_send.at[d],
@@ -152,6 +170,11 @@
         x_copy(kind, z).start()
         y_copy(kind, z).start()
     out_copy().start()
+    blocks = [find(j) for j in range(plane)]
+
+    def chosen(zz, j):
+        return sum(jnp.where(zz == i, got, 0) for i, got in enumerate(blocks[j]))
+
 
     def turn(zz):
         arrive(0, zz * plane + y * NX + 1 - x)
@@ -255,8 +278,8 @@
     edge = 16
 
     def attend(c, start, count):
-        one = slot_ref[KNB * c]
-        two = slot_ref[KNB * c + 1]
+        one = slot_of(KNB * c)
+        two = slot_of(KNB * c + 1)
         last = lax.broadcasted_iota(jnp.int32, (edge, HD), 0) == edge - 1
         batch = 4
         for first in range(0, width // HD, batch):
@@ -347,26 +370,10 @@
 
 def local_small(queries, key_weight, value_weight, out_weight, database, neighbours, placement):
     n = NZ * NY * NX
-    s = lax.axis_index("shard")
     h = lax.axis_index("head")
     tok, width = queries.shape
-    blk, half, de = database.shape
+    half, de = database.shape[1:]
     feats = out_weight.shape[0] // 2
-    nblocks = placement.shape[0]
-    ids = jnp.arange(nblocks, dtype=jnp.int32)
-    needed = neighbours.reshape(n, -1)
-    slots = jnp.sum(jnp.where(needed[:, :, None] == ids, placement, 0), axis=-1)
-    owners = slots // blk
-    offs = jnp.arange(n, dtype=jnp.int32)
-    plane = NY * NX
-    dests = shifted(s, 0, (offs // NX) % NY, offs % NX)
-    origin = offs // plane * plane + s % plane
-    pick = (dests[:, None, None] == offs[None, :, None]) & (owners[None] == origin[:, None, None])
-    which = jnp.sum(jnp.where(pick, (slots % blk)[None], 0), axis=(1, 2))
-    own = jnp.sum(jnp.where((offs == s)[:, None], owners, 0), axis=0)
-    slot = (
-        own // plane * plane + (s // NX + own // NX) % NY * NX + (s + own) % NX
-    ).astype(jnp.int32)
     vm = pl.BlockSpec(memory_space=pltpu.VMEM)
     sm = pl.BlockSpec(memory_space=pltpu.SMEM)
     hbm = pl.BlockSpec(memory_space=pl.ANY)
@@ -392,7 +399,7 @@
         ],
         compiler_params=pltpu.CompilerParams(
             collective_id=0, has_side_effects=True, vmem_limit_bytes=VMEM_LIMIT),
-    )(which.astype(jnp.int32), slot, queries, key_weight, value_weight, out_weight, database)
+    )(neighbours.reshape(-1), placement, queries, key_weight, value_weight, out_weight, database)
     tile = 512
     steps = feats // tile
     return pl.pallas_call(

time: 103 us -> 101 us (0.981)
  other arithmetic: 2.84 us -> 0 us
    reduce_sum x3 -> x0, other arithmetic: 2.18 us -> none  [the longest x1 1.08 us: local_small(): slots = jnp.sum(jnp.where(needed[:, :, None] == ids, placement, 0), axis=-1)]
where the time goes in v4:
time: 101 us
  Pallas kernels  99.5 us (99%)
  local copies, waits for them, and re-layouts  1.49 us (1%)
    pallas_call x1, Pallas kernels, local_small(): pl.pallas_call(fused_kernel, out_shape=(jax.ShapeDtypeStruct((2, tok, wid...  90.7 us
    pallas_call x1, Pallas kernels, local_small(): pl.pallas_call(project_kernel, out_shape=jax.ShapeDtypeStruct((tok, feats...  8.78 us

profile of v4, /device:TPU:0, one launch (start us, length us, event | category | flops | bytes accessed | tf_op | source)
XLA Modules:
  0.0 101.0 jit_solution(12003549165448011795)
XLA Ops:
  0.0 0.8 copy.8
  0.8 0.7 reshape.7.near_ref
  1.5 90.7 %shard_map.73 = (bf16[2,512,1024]{2,1,0:T(8,128)(2,1)}, bf16[2048,1024]{1,0:T(8,128)(2,1)}) custom-call(s32[256]{0:T(256)} %reshape.7.near_ref, s32[64]{0:T(128)} %place_ref.1, bf16[512,1024]{1,0:T(8,128)(2,1)} %q_ref.1, bf16[64,1024]{1,0:T(8,128)(2,1)} %kw_ref.1, bf16[64,1024]{1,0:T(8,128)(2,1)} %vw_ref.1, bf16[4096,1024]{1,0:T(8,128)(2,1)} %own_ref.1, ...), custom_call_target="tpu_custom_call" | custom-call | tf_op jit(solution)/shard_map/pallas_call | solution.py:381
  92.2 8.8 %shard_map.74 = bf16[512,2048]{1,0:T(8,128)(2,1)} custom-call(s32[1]{0:T(128)} %bitcast.side_ref, bf16[2,512,1024]{2,1,0:T(8,128)(2,1)} %get-tuple-element.7.att_ref, bf16[4096,1024]{1,0:T(8,128)(2,1)} %own_ref.1, bf16[2048,1024]{1,0:T(8,128)(2,1)} %get-tuple-element.8.other_ref), custom_call_target="tpu_custom_call" | custom-call | tf_op jit(solution)/shard_map/pallas_call | solution.py:405
